TPU v7x, 128 devices: a whole 4x4x4 slice. The times are simulated.
128 devices in a mesh: req: 32 (over z, y, x_hi), tensor: 4 (over x_lo, core).
Axes of the slice: x: 4 (x_hi: 2, x_lo: 2; x = x_hi * 2 + x_lo), y: 4, z: 4, core: 2. Of those that a mesh axis runs over, the one named last changes fastest.
Arguments:
- span_in: bfloat16 [64, 512, 2048], P('req'), may hold values from -6 to 6
- w_qkv: bfloat16 [3, 2048, 2048], P(None, None, 'tensor'), may hold values from -1 to 1
- qk_gain: bfloat16 [2, 2048], P(None, 'tensor'), may hold values from 0.099609375 to 1.8984375
- w_out: bfloat16 [2048, 2048], P('tensor'), may hold values from -1 to 1
- post_gain: bfloat16 [2048], P('tensor'), may hold values from 0.099609375 to 1.8984375
- kv_pool: bfloat16 [4, 2048, 16, 2048], P(None, 'req', None, 'tensor'), may hold values from -66 to 66
- block_table: int32 [64, 32], replicated, may hold values from 0 to 63, as said below
- request_order: int32 [64], replicated, may hold values from 0 to 63, each once
- lengths: int32 [64], replicated, may hold values from 1 to 512, as said below
Outputs:
- span_out: bfloat16 [64, 512, 2048], P('req', None, 'tensor')
- relaid_cache: bfloat16 [4, 64, 512, 2048], P(None, 'req', None, 'tensor')
Inputs may be any that keep to these rules, and one draw needn't show every extreme that they name: `block_table`: entry (r, j) is the slot, among the 64 slots of the req index j modulo the number of req devices, that holds block j of request r; each slot of each req index is named once. `lengths`: some request has exactly 512 cached tokens.
All inputs are finite; a program needn't handle non-finite values.
Results may differ from a plain program's by a relative error of at most 0.0095.
Values may be sent and summed in bfloat16 or wider, within the bound.
A program may use at most 192 MiB of HBM per device.

v0:
```python
import jax
import jax.numpy as jnp
from jax import lax
from jax.sharding import PartitionSpec as P

HD = 128
norm_eps = 1e-06
rope_base = 500000.0


def rotate(values, positions):
    half_dim = values.shape[-1] // 2
    frequency = rope_base ** (-jnp.arange(half_dim, dtype=jnp.float32) * (2.0 / values.shape[-1]))
    angles = positions[:, None] * frequency[None, :]
    cosine = jnp.cos(angles)[:, None, :]
    sine_part = jnp.sin(angles)[:, None, :]
    first_half = values[..., :half_dim]
    second_half = values[..., half_dim:]
    return jnp.concatenate(
        [
            first_half * cosine - second_half * sine_part,
            second_half * cosine + first_half * sine_part,
        ],
        axis=-1,
    )


def on_device(
    span_in, w_qkv, qk_gain, w_out, post_gain, kv_pool, block_table, request_order, lengths
):
    req_count = lax.axis_size("req")
    req_index = lax.axis_index("req")
    per_device = span_in.shape[0]
    span_len = span_in.shape[1]
    full_width = span_in.shape[2]
    part_width = w_qkv.shape[2]
    block_len = kv_pool.shape[2]
    blocks_each = block_table.shape[1] // req_count
    wanted = jnp.transpose(request_order.reshape(req_count, per_device))
    table_rows = jnp.take(block_table, wanted, axis=0)
    local_blocks = req_index + req_count * jnp.arange(blocks_each, dtype=jnp.int32)
    picked = jnp.take(table_rows, local_blocks, axis=2)
    picked = jnp.transpose(picked, (0, 2, 1)).reshape(-1)
    gathered = jnp.take(kv_pool, picked, axis=1)
    received = lax.all_to_all(
        gathered.reshape(
            kv_pool.shape[0], per_device, blocks_each, req_count * block_len, part_width
        ),
        "req",
        split_axis=3,
        concat_axis=3,
        tiled=True,
    )
    relaid = received.reshape(kv_pool.shape[0], per_device, -1, part_width)
    my_order = lax.dynamic_slice_in_dim(request_order, req_index * per_device, per_device)
    my_lengths = jnp.take(lengths, my_order)
    flat_in = span_in.reshape(-1, full_width)
    projected = jnp.einsum("rd,mdw->mrw", flat_in, w_qkv, preferred_element_type=jnp.float32)
    queries = projected[0]
    keys_new = projected[1]
    values_new = projected[2].astype(jnp.bfloat16)
    query_sq, key_sq = lax.psum(
        (jnp.sum(queries * queries, axis=-1), jnp.sum(keys_new * keys_new, axis=-1)), "tensor"
    )
    norm_gains = qk_gain.astype(jnp.float32)
    queries = queries * lax.rsqrt(query_sq / full_width + norm_eps)[:, None] * norm_gains[0]
    keys_new = keys_new * lax.rsqrt(key_sq / full_width + norm_eps)[:, None] * norm_gains[1]
    positions = (
        my_lengths.astype(jnp.float32)[:, None] + jnp.arange(span_len, dtype=jnp.float32)[None, :]
    ).reshape(-1)
    local_heads = part_width // HD
    query_rot = rotate(queries.reshape(-1, local_heads, HD), positions).astype(jnp.bfloat16)
    query_rot = query_rot.reshape(per_device, span_len, local_heads, HD)
    key_rot = rotate(keys_new.reshape(-1, local_heads, HD), positions).astype(jnp.bfloat16)
    key_rot = key_rot.reshape(per_device, span_len, local_heads, HD)
    context = relaid.shape[2]
    all_keys = jnp.concatenate(
        [relaid[0].reshape(per_device, context, local_heads, HD), key_rot], axis=1
    )
    all_values = jnp.concatenate(
        [
            relaid[1].reshape(per_device, context, local_heads, HD),
            values_new.reshape(per_device, span_len, local_heads, HD),
        ],
        axis=1,
    )
    scores = jnp.einsum(
        "bqhd,bkhd->bhqk", query_rot, all_keys, preferred_element_type=jnp.float32
    ) * HD ** (-0.5)
    cache_live = jnp.arange(context, dtype=jnp.int32)[None, :] < my_lengths[:, None]
    causal = jnp.arange(span_len)[None, :] <= jnp.arange(span_len)[:, None]
    live_mask = jnp.concatenate(
        [
            jnp.broadcast_to(cache_live[:, None, :], (per_device, span_len, context)),
            jnp.broadcast_to(causal[None], (per_device, span_len, span_len)),
        ],
        axis=2,
    )
    scores = jnp.where(live_mask[:, None], scores, -1e30)
    maxima = jnp.max(scores, axis=-1, keepdims=True)
    exponent = jnp.exp(scores - maxima)
    weights = (exponent / jnp.sum(exponent, axis=-1, keepdims=True)).astype(jnp.bfloat16)
    attended = jnp.einsum(
        "bhqk,bkhd->bqhd", weights, all_values, preferred_element_type=jnp.float32
    )
    attended = attended.astype(jnp.bfloat16).reshape(-1, part_width)
    partial_value = jnp.dot(attended, w_out, preferred_element_type=jnp.float32)
    tensor_index = lax.axis_index("tensor")
    residual_part = lax.dynamic_slice_in_dim(
        flat_in, tensor_index * part_width, part_width, 1
    ).astype(jnp.float32)
    gain_part = post_gain.astype(jnp.float32)
    summed = lax.psum(partial_value.astype(jnp.bfloat16), "tensor").astype(jnp.float32)
    scale_rows = lax.rsqrt(jnp.mean(summed * summed, axis=-1, keepdims=True) + norm_eps)
    own_share = lax.dynamic_slice_in_dim(summed, tensor_index * part_width, part_width, 1)
    layer_out = (residual_part + own_share * scale_rows * gain_part).astype(jnp.bfloat16)
    return (layer_out.reshape(per_device, span_len, part_width), relaid)


def solution(mesh):
    placed = (
        P("req", None, None),
        P(None, None, "tensor"),
        P(None, "tensor"),
        P("tensor", None),
        P("tensor"),
        P(None, "req", None, "tensor"),
        P(),
        P(),
        P(),
    )
    return jax.shard_map(
        on_device,
        mesh=mesh,
        in_specs=placed,
        out_specs=(P("req", None, "tensor"), P(None, "req", None, "tensor")),
        check_vma=False,
    )
```

profile of v0, /device:TPU:1, one launch (start us, length us, event | category | flops | bytes accessed | tf_op | source)
XLA Modules:
  0.0 270.8 jit_solution(14465095064436898901)
XLA Ops:
  7.2 0.9 reshape.246
  8.1 0.1 copy.77
  8.2 0.1 copy.78
  8.3 0.1 reshape.292
  8.4 0.8 copy.79
  9.2 0.6 gather_fusion
  9.8 0.1 constant_dynamic-slice_fusion
  9.9 0.1 copy.100
  10.0 0.1 select_n.95
  10.1 0.1 copy.81
  10.2 0.1 copy.84
  10.3 0.1 broadcast_in_dim.91
  10.3 0.1 broadcast_in_dim.92
  10.5 5.0 %gather_fusion.1 = bf16[64,4,16,512]{3,2,1,0:T(8,128)(2,1)} fusion(bf16[4,64,16,512]{3,2,1,0:T(8,128)(2,1)} %param.14, s32[1024]{0:T(1024)S(1)} %pad_clamp_fusion.1), kind=kCustom, calls=%fused_computation.1 | custom fusion | bytes 8388864 | tf_op jit(solution)/shard_map/jit(_take)/gather | solution.py:44
  15.5 2.6 copy.85
  18.1 0.5 broadcast_select_fusion
  18.6 6.3 %copy.86 = bf16[4,2,1,512,512]{4,1,0,2,3:T(2,128)(2,1)} copy(bf16[4,2,1,512,512]{4,3,1,0,2:T(8,128)(2,1)S(1)} %broadcast_select_fusion) | data formatting | bytes 8388608 | tf_op jit(solution)/shard_map/jit(_take)/select_n | solution.py:44
  24.9 11.6 %all-to-all-start = ((bf16[4,2,1,512,512]{4,1,0,2,3:T(2,128)(2,1)}), bf16[4,2,1,512,512]{4,1,0,2,3:T(2,128)(2,1)}, u32[]{:S(2)}, u32[]{:S(2)}) async-start(bf16[4,2,1,512,512]{4,1,0,2,3:T(2,128)(2,1)} %copy.86), calls=%async_computation | async-start | bytes 8388608 | tf_op jit(solution)/shard_map/all_to_all | solution.py:45
  36.5 0.0 all-reduce.3.cloned.1.call-start
  36.6 0.1 compare_select_fusion.2
  36.7 0.6 gather_fusion.2
  37.3 0.1 fusion.31
  37.4 0.1 add_bitcast_fusion
  37.5 10.1 %convolution_bitcast_fusion = f32[3,1024,512]{1,2,0:T(8,128)S(1)} fusion(bf16[3,2048,512]{2,1,0:T(8,128)(2,1)} %param.10, bf16[1024,2048,1]{1,0,2:T(8,128)(2,1)} %bitcast.59), kind=kOutput, calls=%fused_computation.16 | convolution fusion | flops 6442450944 | bytes 16777216 | tf_op jit(solution)/shard_map/rd,mdw->mrw/dot_general | solution.py:58
  47.6 2.6 copy-done.4
  50.2 1.1 slice.84
  51.3 1.8 convert_element_type.42
  53.2 1.1 copy.89
  54.3 5.0 %multiply_reduce_fusion.2 = (f32[1024]{0:T(1024)S(1)}, f32[1024]{0:T(1024)S(1)}, f32[1,1024,512]{1,2,0:T(8,128)}, f32[1,1024,512]{1,2,0:T(8,128)}) fusion(f32[3,1024,512]{1,2,0:T(8,128)} %copy-done.4), kind=kLoop, calls=%fused_computation.31 | loop fusion | flops 2095104 | bytes 8396800 | tf_op jit(solution)/shard_map/reduce_sum | solution.py:63
  59.4 32.4 %all-reduce = (f32[1024]{0:T(1024)S(1)}, f32[1024]{0:T(1024)S(1)}) all-reduce(f32[1024]{0:T(1024)S(1)} %get-tuple-element.18, f32[1024]{0:T(1024)S(1)} %get-tuple-element.17), channel_id=1, replica_groups=mesh['req'=32,'tensor'=4] {'tensor'}, use_global_device_ids=true, to_apply=%region_3.4 | all-reduce | flops 2048 | bytes 16384 | tf_op jit(solution)/shard_map/psum | solution.py:62
  91.8 1.0 multiply_cosine_fusion
  92.8 1.8 multiply_multiply_fusion.1
  94.6 0.2 multiply_multiply_fusion
  94.9 1.9 subtract_convert_fusion.1
  96.8 1.4 concatenate.29
  98.2 1.4 copy.90
  99.6 1.4 concatenate.30
  101.0 1.4 copy.91
  102.4 1.4 concatenate.33
  103.8 1.3 copy.94
  105.1 0.4 concatenate.32
  105.5 1.4 copy.93
  106.9 0.1 iota_compare_fusion
  107.0 0.1 iota_compare_fusion.1
  107.0 0.1 broadcast_in_dim.97
  107.2 0.1 broadcast_in_dim.96
  107.3 1.1 pad_add_fusion
  108.4 3.5 %fusion.32 = (bf16[1,2,1,512,512]{4,1,0,2,3:T(2,128)(2,1)S(1)}, bf16[1,2,1,512,512]{4,1,0,2,3:T(2,128)(2,1)}) fusion(bf16[4,2,1,512,512]{4,1,0,2,3:T(2,128)(2,1)} %all-to-all-done), kind=kLoop, calls=%fused_computation.70 | loop fusion | bytes 4194304 | tf_op jit(solution)/shard_map/slice | solution.py:82
  111.9 2.5 copy.87
  114.3 2.4 copy.99
  116.8 1.3 copy.95
  118.1 10.6 %fusion.9 = f32[2,4,512,1024]{3,2,1,0:T(8,128)} fusion(bf16[2,512,4,64]{3,1,2,0:T(8,128)(2,1)} %copy.94, bf16[2,512,4,64]{3,1,2,0:T(8,128)(2,1)} %copy.93, bf16[2,512,4,128]{3,1,2,0:T(8,128)(2,1)} %copy.95, bf16[2,512,4,64]{3,1,2,0:T(8,128)(2,1)} %copy.91, bf16[2,512,4,64]{3,1,2,0:T(8,128)(2,1)} %copy.90), kind=kOutput, calls=%fused_computation.21 | convolution fusion | flops 1082130432 | bytes 19922944 | tf_op jit(solution)/shard_map/bqhd,bkhd->bhqk/dot_general | solution.py:87
  128.7 22.1 %fusion.34 = (f32[2,4,512]{2,1,0:T(4,128)S(1)}, f32[2,4,512,1024]{3,2,1,0:T(8,128)}) fusion(f32[2,4,512,1024]{3,2,1,0:T(8,128)} %fusion.9, pred[2,512,1024]{2,1,0:T(8,128)(4,1)} %pad_add_fusion), kind=kOutput, calls=%fused_computation.72 | output fusion | flops 25166848 | bytes 34619392 | tf_op jit(solution)/shard_map/sub | solution.py:101
  150.8 8.5 %fusion.18 = bf16[2,512,4,128]{1,3,2,0:T(8,128)(2,1)} fusion(f32[2,4,512,1024]{3,2,1,0:T(8,128)} %get-tuple-element.38, f32[2,4,512]{2,1,0:T(4,128)S(1)} %get-tuple-element.37, bf16[2,512,4,128]{1,3,2,0:T(8,128)(2,1)S(1)} %copy-done.5, bf16[2,512,4,128]{1,3,2,0:T(8,128)(2,1)} %bitcast.57), kind=kOutput, calls=%fused_computation.33 | convolution fusion | flops 1086849024 | bytes 19939328 | tf_op jit(solution)/shard_map/bhqk,bkhd->bqhd/dot_general | solution.py:103
  159.3 1.7 copy.96
  161.0 4.3 %convolution_convert_fusion = bf16[1024,2048]{1,0:T(8,128)(2,1)} fusion(bf16[512,2048]{1,0:T(8,128)(2,1)S(1)} %copy-done, bf16[128,8,4,128]{3,2,1,0:T(4,128)(2,1)S(1)} %bitcast.58), kind=kOutput, calls=%fused_computation.15 | convolution fusion | flops 2149580800 | bytes 7340032 | tf_op jit(solution)/shard_map/dot_general | solution.py:107
  165.4 0.0 all-reduce.3.cloned.1.call-update
  165.4 0.6 copy-done.8
  166.0 5.7 %copy.97 = bf16[4,2,512,512]{3,2,1,0:T(8,128)(2,1)} copy(bf16[4,2,512,512]{3,1,0,2:T(2,128)(2,1)} %bitcast.20) | data formatting | bytes 8388608
  171.7 85.1 %all-reduce.3.cloned.1.call-done = bf16[1024,2048]{1,0:T(8,128)(2,1)} async-done(((bf16[1024,2048]{1,0:T(8,128)(2,1)}), bf16[1024,2048]{1,0:T(8,128)(2,1)}) %all-reduce.3.cloned.1.call-update) | async-done | bytes 4194320 | tf_op jit(solution)/shard_map/psum | solution.py:113
  256.8 3.2 %multiply_reduce_fusion = f32[1024]{0:T(1024)S(1)} fusion(bf16[1024,2048]{1,0:T(8,128)(2,1)} %all-reduce.3.cloned.1.call-done), kind=kLoop, calls=%fused_computation.8 | loop fusion | flops 6290432 | bytes 4198400 | tf_op jit(solution)/shard_map/reduce_sum | solution.py:114
  260.1 0.2 copy-done.2
  260.3 1.1 convert_element_type.49
  261.4 2.6 add_convert_fusion
  (30 shorter events, 0.1 us)
Async XLA Ops:
  7.2 153.9 %copy-start = (bf16[512,2048]{1,0:T(8,128)(2,1)S(1)}, bf16[512,2048]{1,0:T(8,128)(2,1)}, u32[]{:S(2)}) copy-start(bf16[512,2048]{1,0:T(8,128)(2,1)} %param.12) | copy-start | bytes 6291460
  24.9 11.7 %copy-start.7 = (s32[64]{0:T(128)S(1)}, s32[64]{0:T(128)}, u32[]{:S(2)}) copy-start(s32[64]{0:T(128)} %param.16) | copy-start | bytes 772
  24.9 11.8 %copy-start.1 = (s32[64]{0:T(128)S(1)}, s32[64]{0:T(128)}, u32[]{:S(2)}) copy-start(s32[64]{0:T(128)} %param.17) | copy-start | bytes 772
  24.9 83.5 %all-to-all-start = ((bf16[4,2,1,512,512]{4,1,0,2,3:T(2,128)(2,1)}), bf16[4,2,1,512,512]{4,1,0,2,3:T(2,128)(2,1)}, u32[]{:S(2)}, u32[]{:S(2)}) async-start(bf16[4,2,1,512,512]{4,1,0,2,3:T(2,128)(2,1)} %copy.86), calls=%async_computation | async-start | bytes 8388608 | tf_op jit(solution)/shard_map/all_to_all | solution.py:45
  36.5 220.3 %all-reduce.3.cloned.1.call-start = ((), (), s32[]{:S(2)}) async-start(), calls=%async_computation.1 | async-start | bytes 8388608 | tf_op jit(solution)/shard_map/psum | solution.py:113
  47.6 2.6 copy-start.4
  54.3 37.4 %copy-start.6 = (bf16[2,512]{1,0:T(2,128)(2,1)S(1)}, bf16[2,512]{1,0:T(2,128)(2,1)}, u32[]{:S(2)}) copy-start(bf16[2,512]{1,0:T(2,128)(2,1)} %param.11) | copy-start | bytes 6148
  91.7 2.9 %copy-start.3 = (f32[1,1024,512]{1,2,0:T(8,128)S(1)}, f32[1,1024,512]{1,2,0:T(8,128)}, u32[]{:S(2)}) copy-start(f32[1,1024,512]{1,2,0:T(8,128)} %get-tuple-element.24) | copy-start | bytes 6291460
  128.7 22.1 %copy-start.5 = (bf16[2,512,4,128]{1,3,2,0:T(8,128)(2,1)S(1)}, bf16[2,512,4,128]{1,3,2,0:T(8,128)(2,1)}, u32[]{:S(2)}) copy-start(bf16[2,512,4,128]{1,3,2,0:T(8,128)(2,1)} %copy.89) | copy-start | bytes 3145732
  165.4 0.7 copy-start.8
  256.8 3.4 %copy-start.2 = (bf16[1024,2048]{1,0:T(8,128)(2,1)S(1)}, bf16[1024,2048]{1,0:T(8,128)(2,1)}, u32[]{:S(2)}) copy-start(bf16[1024,2048]{1,0:T(8,128)(2,1)} %all-reduce.3.cloned.1.call-done) | copy-start | bytes 12582916
Sparse Core Ops, SparseCore 0:
  165.5 91.2 all-reduce.2
where the time goes:
time: 271 us
  waiting for transfers between devices  85.2 us (31%)
  local copies, waits for them, and re-layouts  52.8 us (19%)
  other arithmetic  41 us (15%)
  matrix products  33.6 us (12%)
  blocking collectives  32.4 us (12%)
  between operations  14.3 us (5%)
  starting transfers between devices  11.6 us (4%)
    psum x1, waiting for transfers between devices, on_device(): lax.psum(partial_value.astype(jnp.bfloat16), 'tensor').astype(jnp.float32)  85.1 us
    psum x1, blocking collectives, on_device(): lax.psum((jnp.sum(queries * queries, axis=-1), jnp.sum(keys_new * keys_ne...  32.4 us
    sub x1, other arithmetic, on_device(): exponent = jnp.exp(scores - maxima)  22.1 us
    unnamed x23, local copies, waits for them, and re-layouts  12.5 us
    all_to_all x1, starting transfers between devices, on_device(): lax.all_to_all(gathered.reshape(kv_pool.shape[0], per_device, blocks_each...  11.6 us
    dot_general x1, matrix products, on_device(): jnp.einsum('bqhd,bkhd->bhqk', query_rot, all_keys, preferred_element_type...  10.6 us
    dot_general x1, matrix products, on_device(): jnp.einsum('rd,mdw->mrw', flat_in, w_qkv, preferred_element_type=jnp.floa...  10.1 us
    concatenate x8, local copies, waits for them, and re-layouts, rotate(): jnp.concatenate([first_half * cosine - second_half * sine_part, second_ha...  10 us
  transfers between devices with their start and end apart: 2, of which 1 were waited for; matrix products, arithmetic and copies ran while one was open for 16% of the time, Pallas kernels for 0%

commit v1 on v0

--- a/solution.py
+++ b/solution.py
@@ -110,7 +110,9 @@
         flat_in, tensor_index * part_width, part_width, 1
     ).astype(jnp.float32)
     gain_part = post_gain.astype(jnp.float32)
-    summed = lax.psum(partial_value.astype(jnp.bfloat16), "tensor").astype(jnp.float32)
+    summed = jnp.sum(lax.all_gather(partial_value.astype(jnp.bfloat16), "tensor"), axis=0).astype(
+        jnp.float32
+    )
     scale_rows = lax.rsqrt(jnp.mean(summed * summed, axis=-1, keepdims=True) + norm_eps)
     own_share = lax.dynamic_slice_in_dim(summed, tensor_index * part_width, part_width, 1)
     layer_out = (residual_part + own_share * scale_rows * gain_part).astype(jnp.bfloat16)

time: 271 us -> 343 us (1.27)
  waiting for transfers between devices: 85.2 us -> 145 us
  other arithmetic: 41 us -> 53 us
    all_gather x0 -> x1, waiting for transfers between devices: none -> 145 us  [on_device(): lax.all_gather(partial_value.astype(jnp.bfloat16), 'tensor')]
    psum x1 -> x0, waiting for transfers between devices: 85.1 us -> none  [on_device(): lax.psum(partial_value.astype(jnp.bfloat16), 'tensor').astype(jnp.float32)]
    reduce_sum x0 -> x1, other arithmetic: none -> 12 us  [on_device(): jnp.sum(lax.all_gather(partial_value.astype(jnp.bfloat16), 'tensor'), axi...]
  transfers between devices with their start and end apart: 2 -> 2, of which waited for: 1 -> 1; matrix products, arithmetic and copies ran while one was open for 16% -> 12% of each run, Pallas kernels for 0% -> 0%
where the time goes in v1:
time: 343 us
  waiting for transfers between devices  145 us (42%)
  other arithmetic  53 us (15%)
  local copies, waits for them, and re-layouts  52.8 us (15%)
  matrix products  33.5 us (10%)
  blocking collectives  32.4 us (9%)
  between operations  14.3 us (4%)
  starting transfers between devices  11.6 us (3%)
    all_gather x1, waiting for transfers between devices, on_device(): lax.all_gather(partial_value.astype(jnp.bfloat16), 'tensor')  145 us
    psum x1, blocking collectives, on_device(): lax.psum((jnp.sum(queries * queries, axis=-1), jnp.sum(keys_new * keys_ne...  32.4 us
    sub x1, other arithmetic, on_device(): exponent = jnp.exp(scores - maxima)  22.1 us
    unnamed x23, local copies, waits for them, and re-layouts  12.6 us
    reduce_sum x1, other arithmetic, on_device(): jnp.sum(lax.all_gather(partial_value.astype(jnp.bfloat16), 'tensor'), axi...  12 us
    all_to_all x1, starting transfers between devices, on_device(): lax.all_to_all(gathered.reshape(kv_pool.shape[0], per_device, blocks_each...  11.6 us
    dot_general x1, matrix products, on_device(): jnp.einsum('bqhd,bkhd->bhqk', query_rot, all_keys, preferred_element_type...  10.6 us
    dot_general x1, matrix products, on_device(): jnp.einsum('rd,mdw->mrw', flat_in, w_qkv, preferred_element_type=jnp.floa...  10.1 us
  transfers between devices with their start and end apart: 2, of which 1 were waited for; matrix products, arithmetic and copies ran while one was open for 12% of the time, Pallas kernels for 0%

profile of v1, /device:TPU:1, one launch (start us, length us, event | category | flops | bytes accessed | tf_op | source)
XLA Modules:
  0.0 342.5 jit_solution(1354265447396721570)
XLA Ops:
  7.2 0.9 reshape.246
  8.1 0.1 copy.77
  8.2 0.1 copy.78
  8.3 0.1 reshape.292
  8.4 0.8 copy.79
  9.2 0.6 gather_fusion
  9.8 0.1 constant_dynamic-slice_fusion
  9.9 0.1 copy.100
  10.0 0.1 select_n.95
  10.1 0.1 copy.81
  10.2 0.1 copy.84
  10.3 0.1 broadcast_in_dim.91
  10.3 0.1 broadcast_in_dim.92
  10.5 5.0 %gather_fusion.1 = bf16[64,4,16,512]{3,2,1,0:T(8,128)(2,1)} fusion(bf16[4,64,16,512]{3,2,1,0:T(8,128)(2,1)} %param.14, s32[1024]{0:T(1024)S(1)} %pad_clamp_fusion.1), kind=kCustom, calls=%fused_computation.1 | custom fusion | bytes 8388864 | tf_op jit(solution)/shard_map/jit(_take)/gather | solution.py:44
  15.5 2.6 copy.85
  18.1 0.5 broadcast_select_fusion
  18.6 6.3 %copy.86 = bf16[4,2,1,512,512]{4,1,0,2,3:T(2,128)(2,1)} copy(bf16[4,2,1,512,512]{4,3,1,0,2:T(8,128)(2,1)S(1)} %broadcast_select_fusion) | data formatting | bytes 8388608 | tf_op jit(solution)/shard_map/jit(_take)/select_n | solution.py:44
  24.9 11.6 %all-to-all-start = ((bf16[4,2,1,512,512]{4,1,0,2,3:T(2,128)(2,1)}), bf16[4,2,1,512,512]{4,1,0,2,3:T(2,128)(2,1)}, u32[]{:S(2)}, u32[]{:S(2)}) async-start(bf16[4,2,1,512,512]{4,1,0,2,3:T(2,128)(2,1)} %copy.86), calls=%async_computation | async-start | bytes 8388608 | tf_op jit(solution)/shard_map/all_to_all | solution.py:45
  36.5 0.0 all-gather.3.cloned.1.call-start
  36.6 0.1 compare_select_fusion.2
  36.7 0.6 gather_fusion.2
  37.3 0.1 fusion.31
  37.4 0.1 add_bitcast_fusion
  37.5 10.1 %convolution_bitcast_fusion = f32[3,1024,512]{1,2,0:T(8,128)S(1)} fusion(bf16[3,2048,512]{2,1,0:T(8,128)(2,1)} %param.10, bf16[1024,2048,1]{1,0,2:T(8,128)(2,1)} %bitcast.61), kind=kOutput, calls=%fused_computation.16 | convolution fusion | flops 6442450944 | bytes 16777216 | tf_op jit(solution)/shard_map/rd,mdw->mrw/dot_general | solution.py:58
  47.6 2.6 copy-done.4
  50.2 1.1 slice.84
  51.3 1.8 convert_element_type.44
  53.2 1.1 copy.89
  54.3 5.0 %multiply_reduce_fusion.2 = (f32[1024]{0:T(1024)S(1)}, f32[1024]{0:T(1024)S(1)}, f32[1,1024,512]{1,2,0:T(8,128)}, f32[1,1024,512]{1,2,0:T(8,128)}) fusion(f32[3,1024,512]{1,2,0:T(8,128)} %copy-done.4), kind=kLoop, calls=%fused_computation.31 | loop fusion | flops 2095104 | bytes 8396800 | tf_op jit(solution)/shard_map/reduce_sum | solution.py:63
  59.4 32.4 %all-reduce = (f32[1024]{0:T(1024)S(1)}, f32[1024]{0:T(1024)S(1)}) all-reduce(f32[1024]{0:T(1024)S(1)} %get-tuple-element.18, f32[1024]{0:T(1024)S(1)} %get-tuple-element.17), channel_id=1, replica_groups=mesh['req'=32,'tensor'=4] {'tensor'}, use_global_device_ids=true, to_apply=%region_3.4 | all-reduce | flops 2048 | bytes 16384 | tf_op jit(solution)/shard_map/psum | solution.py:62
  91.8 1.0 multiply_cosine_fusion
  92.8 1.8 multiply_multiply_fusion.1
  94.6 0.2 multiply_multiply_fusion
  94.9 1.9 subtract_convert_fusion.1
  96.8 1.4 concatenate.29
  98.2 1.4 copy.90
  99.6 1.4 concatenate.30
  101.0 1.4 copy.91
  102.4 1.4 concatenate.33
  103.8 1.3 copy.94
  105.1 0.4 concatenate.32
  105.5 1.4 copy.93
  106.9 0.1 iota_compare_fusion
  107.0 0.1 iota_compare_fusion.1
  107.0 0.1 broadcast_in_dim.97
  107.2 0.1 broadcast_in_dim.96
  107.3 1.1 pad_add_fusion
  108.4 3.5 %fusion.32 = (bf16[1,2,1,512,512]{4,1,0,2,3:T(2,128)(2,1)S(1)}, bf16[1,2,1,512,512]{4,1,0,2,3:T(2,128)(2,1)}) fusion(bf16[4,2,1,512,512]{4,1,0,2,3:T(2,128)(2,1)} %all-to-all-done), kind=kLoop, calls=%fused_computation.70 | loop fusion | bytes 4194304 | tf_op jit(solution)/shard_map/slice | solution.py:82
  111.9 2.5 copy.87
  114.3 2.4 copy.99
  116.8 1.3 copy.95
  118.1 10.6 %fusion.9 = f32[2,4,512,1024]{3,2,1,0:T(8,128)} fusion(bf16[2,512,4,64]{3,1,2,0:T(8,128)(2,1)} %copy.94, bf16[2,512,4,64]{3,1,2,0:T(8,128)(2,1)} %copy.93, bf16[2,512,4,128]{3,1,2,0:T(8,128)(2,1)} %copy.95, bf16[2,512,4,64]{3,1,2,0:T(8,128)(2,1)} %copy.91, bf16[2,512,4,64]{3,1,2,0:T(8,128)(2,1)} %copy.90), kind=kOutput, calls=%fused_computation.21 | convolution fusion | flops 1082130432 | bytes 19922944 | tf_op jit(solution)/shard_map/bqhd,bkhd->bhqk/dot_general | solution.py:87
  128.7 22.1 %fusion.34 = (f32[2,4,512]{2,1,0:T(4,128)S(1)}, f32[2,4,512,1024]{3,2,1,0:T(8,128)}) fusion(f32[2,4,512,1024]{3,2,1,0:T(8,128)} %fusion.9, pred[2,512,1024]{2,1,0:T(8,128)(4,1)} %pad_add_fusion), kind=kOutput, calls=%fused_computation.72 | output fusion | flops 25166848 | bytes 34619392 | tf_op jit(solution)/shard_map/sub | solution.py:101
  150.8 8.5 %fusion.18 = bf16[2,512,4,128]{1,3,2,0:T(8,128)(2,1)} fusion(f32[2,4,512,1024]{3,2,1,0:T(8,128)} %get-tuple-element.38, f32[2,4,512]{2,1,0:T(4,128)S(1)} %get-tuple-element.37, bf16[2,512,4,128]{1,3,2,0:T(8,128)(2,1)S(1)} %copy-done.5, bf16[2,512,4,128]{1,3,2,0:T(8,128)(2,1)} %bitcast.59), kind=kOutput, calls=%fused_computation.33 | convolution fusion | flops 1086849024 | bytes 19939328 | tf_op jit(solution)/shard_map/bhqk,bkhd->bqhd/dot_general | solution.py:103
  159.3 1.7 copy.96
  161.0 4.3 %convolution_convert_fusion = bf16[1024,2048]{1,0:T(8,128)(2,1)} fusion(bf16[512,2048]{1,0:T(8,128)(2,1)S(1)} %copy-done, bf16[128,8,4,128]{3,2,1,0:T(4,128)(2,1)S(1)} %bitcast.60), kind=kOutput, calls=%fused_computation.15 | convolution fusion | flops 2149580800 | bytes 7340032 | tf_op jit(solution)/shard_map/dot_general | solution.py:107
  165.3 0.6 copy-done.8
  166.0 5.7 %copy.97 = bf16[4,2,512,512]{3,2,1,0:T(8,128)(2,1)} copy(bf16[4,2,512,512]{3,1,0,2:T(2,128)(2,1)} %bitcast.21) | data formatting | bytes 8388608
  171.7 144.9 %all-gather.3.cloned.1.call-done = bf16[4096,2048]{1,0:T(8,128)(2,1)} async-done(((bf16[1024,2048]{1,0:T(8,128)(2,1)}), bf16[4096,2048]{1,0:T(8,128)(2,1)}) %all-gather.3.cloned.1.call-update) | async-done | bytes 16777232 | tf_op jit(solution)/shard_map/all_gather | solution.py:113
  316.5 12.0 %reduce_sum.51 = bf16[1024,2048]{1,0:T(8,128)(2,1)} reduce(bf16[4,1024,2048]{2,1,0:T(8,128)(2,1)} %bitcast.53, bf16[]{:T(256)} %constant.96.clone.1), dimensions={0}, to_apply=%region_6.7 | reduce | flops 6291456 | bytes 20971522 | tf_op jit(solution)/shard_map/reduce_sum | solution.py:113
  328.6 3.2 multiply_reduce_fusion
  331.8 0.2 copy-done.2
  332.0 1.1 convert_element_type.51
  333.1 2.6 add_convert_fusion
  (31 shorter events, 0.2 us)
Async XLA Ops:
  7.2 153.9 %copy-start = (bf16[512,2048]{1,0:T(8,128)(2,1)S(1)}, bf16[512,2048]{1,0:T(8,128)(2,1)}, u32[]{:S(2)}) copy-start(bf16[512,2048]{1,0:T(8,128)(2,1)} %param.12) | copy-start | bytes 6291460
  24.9 11.7 %copy-start.7 = (s32[64]{0:T(128)S(1)}, s32[64]{0:T(128)}, u32[]{:S(2)}) copy-start(s32[64]{0:T(128)} %param.16) | copy-start | bytes 772
  24.9 11.8 %copy-start.1 = (s32[64]{0:T(128)S(1)}, s32[64]{0:T(128)}, u32[]{:S(2)}) copy-start(s32[64]{0:T(128)} %param.17) | copy-start | bytes 772
  24.9 83.5 %all-to-all-start = ((bf16[4,2,1,512,512]{4,1,0,2,3:T(2,128)(2,1)}), bf16[4,2,1,512,512]{4,1,0,2,3:T(2,128)(2,1)}, u32[]{:S(2)}, u32[]{:S(2)}) async-start(bf16[4,2,1,512,512]{4,1,0,2,3:T(2,128)(2,1)} %copy.86), calls=%async_computation | async-start | bytes 8388608 | tf_op jit(solution)/shard_map/all_to_all | solution.py:45
  36.5 280.0 %all-gather.3.cloned.1.call-start = ((), (), s32[]{:S(2)}) async-start(), calls=%async_computation.1 | async-start | bytes 20971520 | tf_op jit(solution)/shard_map/all_gather | solution.py:113
  47.6 2.6 copy-start.4
  54.3 37.4 %copy-start.6 = (bf16[2,512]{1,0:T(2,128)(2,1)S(1)}, bf16[2,512]{1,0:T(2,128)(2,1)}, u32[]{:S(2)}) copy-start(bf16[2,512]{1,0:T(2,128)(2,1)} %param.11) | copy-start | bytes 6148
  91.7 2.9 copy-start.3
  128.7 22.1 %copy-start.5 = (bf16[2,512,4,128]{1,3,2,0:T(8,128)(2,1)S(1)}, bf16[2,512,4,128]{1,3,2,0:T(8,128)(2,1)}, u32[]{:S(2)}) copy-start(bf16[2,512,4,128]{1,3,2,0:T(8,128)(2,1)} %copy.89) | copy-start | bytes 3145732
  165.3 0.7 copy-start.8
  328.6 3.4 %copy-start.2 = (bf16[1024,2048]{1,0:T(8,128)(2,1)S(1)}, bf16[1024,2048]{1,0:T(8,128)(2,1)}, u32[]{:S(2)}) copy-start(bf16[1024,2048]{1,0:T(8,128)(2,1)} %reduce_sum.51) | copy-start | bytes 12582916
Sparse Core Ops, SparseCore 0:
  165.5 151.0 all-gather.2
